TPU v7x, 32 devices: a whole 2x2x4 slice. The times are simulated.
32 devices in a mesh: fsdp: 2 (over x), context: 4 (over y, core), tensor: 4 (over z).
Axes of the slice: x: 2, y: 2, z: 4, core: 2. Of those that a mesh axis runs over, the one named last changes fastest.
Arguments:
- tokens: bfloat16 [2, 2048, 1024], P('fsdp', 'context'), may hold values from -6 to 6
- cotangent: bfloat16 [2, 2048, 1024], P('fsdp', 'context'), may hold values from -6 to 6
- lengths: int32 [2, 4], P('fsdp'), may hold values from 1 to 1024, 2048 in all within a row
- w_in: bfloat16 [3, 1024, 1024], P(None, 'fsdp', 'tensor'), may hold values from -0.1875 to 0.1875
- w_out: bfloat16 [1024, 1024], P('tensor', 'fsdp'), may hold values from -0.1875 to 0.1875
- w_gate_up: bfloat16 [2, 1024, 4608], P(None, 'fsdp', 'tensor'), may hold values from -0.1875 to 0.1875
- w_down: bfloat16 [4608, 1024], P('tensor', 'fsdp'), may hold values from -0.1875 to 0.1875
- norm_gains: bfloat16 [2, 1024], P(None, 'fsdp'), may hold values from 0.5 to 1.5
- conv_kernel: bfloat16 [3, 1024], P(None, 'tensor'), may hold values from -3 to 3
Outputs:
- block_out: float32 [2, 2048, 1024], P('fsdp', 'context')
- grad_tokens: float32 [2, 2048, 1024], P('fsdp', 'context')
- grad_w_in: float32 [3, 1024, 1024], P(None, 'fsdp', 'tensor')
- grad_w_out: float32 [1024, 1024], P('tensor', 'fsdp')
- grad_w_gate_up: float32 [2, 1024, 4608], P(None, 'fsdp', 'tensor')
- grad_w_down: float32 [4608, 1024], P('tensor', 'fsdp')
- grad_norm_gains: float32 [2, 1024], P(None, 'fsdp')
- grad_conv_kernel: float32 [3, 1024], P(None, 'tensor')
Inputs may be any that keep to these rules, and one draw needn't show every extreme that they name: `lengths`: each row of 2048 tokens is a pack of 4 whole documents, in order; some document of every row has 1024 tokens.
All inputs are finite; a program needn't handle non-finite values.
Results may differ from a plain program's by a relative error of at most 0.0088.
Values may be sent and summed in bfloat16 or wider, within the bound.
No kernel may reach another device: no remote copies, remote signals or barrier semaphores. Data moves between devices by JAX's collectives and lax.ppermute only.
A program may use at most 128 MiB of HBM per device.

v0:
```python
import jax
import jax.numpy as jnp
from jax import lax
from jax.sharding import PartitionSpec as P

norm_eps = 1e-05


def shifted(block, axis, distance):
    devices = range(lax.axis_size(axis))
    route = [(i - distance, i) for i in devices if i - distance in devices]
    return lax.ppermute(block, axis, route)


def matmul_plain(matrix_one, matrix_two):
    return jnp.dot(matrix_one, matrix_two, preferred_element_type=jnp.float32)


def matmul_right(matrix_one, matrix_two):
    return lax.dot_general(
        matrix_one, matrix_two, (((1,), (1,)), ((), ())), preferred_element_type=jnp.float32
    )


def matmul_left(matrix_one, matrix_two):
    return lax.dot_general(
        matrix_one, matrix_two, (((0,), (0,)), ((), ())), preferred_element_type=jnp.float32
    )


def norm_forward(values):
    inv_root = lax.rsqrt(jnp.mean(values * values, axis=-1, keepdims=True) + norm_eps)
    return (values * inv_root, inv_root)


def norm_backward(normed, inv_root, gain_row, grad_out):
    grad_normed = grad_out * gain_row
    inner_mean = jnp.mean(grad_normed * normed, axis=-1, keepdims=True)
    return (inv_root * (grad_normed - normed * inner_mean), jnp.sum(grad_out * normed, axis=0))


def keep_masks(position, lengths_row):
    starts = jnp.cumsum(lengths_row) - lengths_row
    doc_start = jnp.max(jnp.where(starts[None, :] <= position[:, None], starts[None, :], 0), axis=1)
    keep_one = (position - 1 >= doc_start).astype(jnp.float32)[:, None]
    keep_two = (position - 2 >= doc_start).astype(jnp.float32)[:, None]
    return (keep_one, keep_two)


def local(tokens, cotangent, lengths, w_in, w_out, w_gate_up, w_down, norm_gains, conv_kernel):
    block_rows = tokens.shape[1]
    position = lax.axis_index("context") * block_rows + jnp.arange(block_rows + 2, dtype=jnp.int32)
    keep_one_ext, keep_two_ext = keep_masks(position, lengths[0])
    keep_one = keep_one_ext[:block_rows]
    keep_two = keep_two_ext[:block_rows]
    full_in, full_out, full_gate_up, full_down, full_gains = (
        lax.all_gather(w_in, "fsdp", axis=1, tiled=True),
        lax.all_gather(w_out, "fsdp", axis=1, tiled=True),
        lax.all_gather(w_gate_up, "fsdp", axis=1, tiled=True),
        lax.all_gather(w_down, "fsdp", axis=1, tiled=True),
        lax.all_gather(norm_gains, "fsdp", axis=1, tiled=True),
    )
    inputs = tokens[0].astype(jnp.float32)
    gain_first = full_gains[0].astype(jnp.float32)
    gain_second = full_gains[1].astype(jnp.float32)
    kernel_taps = conv_kernel.astype(jnp.float32)
    normed_one, root_one = norm_forward(inputs)
    hidden_one = (normed_one * gain_first).astype(jnp.bfloat16)
    b_part = matmul_plain(hidden_one, full_in[0])
    c_part = matmul_plain(hidden_one, full_in[1])
    x_part = matmul_plain(hidden_one, full_in[2])
    mixed = b_part * x_part
    rim_rows = shifted(mixed[-2:], "context", 1)
    extended = jnp.concatenate([rim_rows, mixed], axis=0)
    back_one = extended[1:-1] * keep_one
    back_two = extended[:-2] * keep_two
    conv_value = kernel_taps[2] * mixed + kernel_taps[1] * back_one + kernel_taps[0] * back_two
    gated = (c_part * conv_value).astype(jnp.bfloat16)
    first_sum = inputs + lax.psum(matmul_plain(gated, full_out), "tensor")
    normed_two, root_two = norm_forward(first_sum)
    hidden_two = (normed_two * gain_second).astype(jnp.bfloat16)
    gate_value = matmul_plain(hidden_two, full_gate_up[0])
    up_value = matmul_plain(hidden_two, full_gate_up[1])
    sigmoid_gate = jax.nn.sigmoid(gate_value)
    silu_gate = gate_value * sigmoid_gate
    act_value = (silu_gate * up_value).astype(jnp.bfloat16)
    output_rows = first_sum + lax.psum(matmul_plain(act_value, full_down), "tensor")
    full_in, full_out, full_gate_up, full_down, full_gains = (
        lax.all_gather(w_in, "fsdp", axis=1, tiled=True),
        lax.all_gather(w_out, "fsdp", axis=1, tiled=True),
        lax.all_gather(w_gate_up, "fsdp", axis=1, tiled=True),
        lax.all_gather(w_down, "fsdp", axis=1, tiled=True),
        lax.all_gather(norm_gains, "fsdp", axis=1, tiled=True),
    )
    cot_rows = cotangent[0]
    grad_act = matmul_right(cot_rows, full_down)
    grad_gate = (
        grad_act * up_value * sigmoid_gate * (1.0 + gate_value * (1.0 - sigmoid_gate))
    ).astype(jnp.bfloat16)
    grad_up = (grad_act * silu_gate).astype(jnp.bfloat16)
    grad_h2 = lax.psum(
        matmul_right(grad_gate, full_gate_up[0]) + matmul_right(grad_up, full_gate_up[1]), "tensor"
    )
    back_second, grad_gain_two = norm_backward(normed_two, root_two, gain_second, grad_h2)
    grad_first = cot_rows.astype(jnp.float32) + back_second
    grad_first_b = grad_first.astype(jnp.bfloat16)
    grad_gated = matmul_right(grad_first_b, full_out)
    grad_conv = grad_gated * c_part
    next_rows = shifted(grad_conv[:2], "context", -1)
    ahead = jnp.concatenate([grad_conv, next_rows], axis=0)
    ahead_one = ahead[1 : block_rows + 1] * keep_one_ext[1 : block_rows + 1]
    ahead_two = ahead[2:] * keep_two_ext[2:]
    grad_mixed = (
        kernel_taps[2] * grad_conv + kernel_taps[1] * ahead_one + kernel_taps[0] * ahead_two
    )
    grad_kernel = jnp.stack(
        [
            jnp.sum(grad_conv * back_two, axis=0),
            jnp.sum(grad_conv * back_one, axis=0),
            jnp.sum(grad_conv * mixed, axis=0),
        ]
    )
    grad_b = (grad_mixed * x_part).astype(jnp.bfloat16)
    grad_c = (grad_gated * conv_value).astype(jnp.bfloat16)
    grad_x = (grad_mixed * b_part).astype(jnp.bfloat16)
    local_h1 = (
        matmul_right(grad_b, full_in[0])
        + matmul_right(grad_c, full_in[1])
        + matmul_right(grad_x, full_in[2])
    )
    grad_h1 = lax.psum(local_h1, "tensor")
    back_first, grad_gain_one = norm_backward(normed_one, root_one, gain_first, grad_h1)
    grad_inputs = grad_first + back_first
    term_in = jnp.stack(
        [
            matmul_left(hidden_one, grad_b),
            matmul_left(hidden_one, grad_c),
            matmul_left(hidden_one, grad_x),
        ]
    )
    term_out = matmul_left(gated, grad_first_b)
    term_gate_up = jnp.stack([matmul_left(hidden_two, grad_gate), matmul_left(hidden_two, grad_up)])
    term_down = matmul_left(act_value, cot_rows)
    term_gains = jnp.stack([grad_gain_one, grad_gain_two])
    pieces = (
        lax.psum_scatter(term_in, "fsdp", scatter_dimension=1, tiled=True),
        lax.psum_scatter(term_out, "fsdp", scatter_dimension=1, tiled=True),
        lax.psum_scatter(term_gate_up, "fsdp", scatter_dimension=1, tiled=True),
        lax.psum_scatter(term_down, "fsdp", scatter_dimension=1, tiled=True),
        lax.psum_scatter(term_gains, "fsdp", scatter_dimension=1, tiled=True),
    )
    reduced = lax.psum((pieces[0], pieces[1], pieces[2], pieces[3], pieces[4]), "context")
    kernel_total = lax.psum(grad_kernel, ("fsdp", "context"))
    return (
        output_rows[None],
        grad_inputs[None],
        reduced[0],
        reduced[1],
        reduced[2],
        reduced[3],
        reduced[4],
        kernel_total,
    )


def solution(mesh):
    placed = (
        P("fsdp", "context", None),
        P("fsdp", "context", None),
        P("fsdp", None),
        P(None, "fsdp", "tensor"),
        P("tensor", "fsdp"),
        P(None, "fsdp", "tensor"),
        P("tensor", "fsdp"),
        P(None, "fsdp"),
        P(None, "tensor"),
    )
    return jax.shard_map(
        local,
        mesh=mesh,
        in_specs=placed,
        out_specs=(
            P("fsdp", "context", None),
            P("fsdp", "context", None),
            P(None, "fsdp", "tensor"),
            P("tensor", "fsdp"),
            P(None, "fsdp", "tensor"),
            P("tensor", "fsdp"),
            P(None, "fsdp"),
            P(None, "tensor"),
        ),
        check_vma=False,
    )
```

profile of v0, /device:TPU:0, one launch (start us, length us, event | category | flops | bytes accessed | tf_op | source)
XLA Modules:
  0.0 958.6 jit_solution(321070914398784171)
XLA Ops:
  9.4 5.5 all_gather.19
  17.5 21.9 %all-gather.4.cloned.1.call-done = bf16[3,1024,256]{2,1,0:T(8,128)(2,1)} async-done(((bf16[3,512,256]{2,1,0:T(8,128)(2,1)}), bf16[3,1024,256]{2,1,0:T(8,128)(2,1)}) %all-gather.4.cloned.1.call-update) | async-done | bytes 1572880 | tf_op jit(solution)/shard_map/all_gather | solution.py:57
  44.4 8.9 all_gather.21
  58.7 84.5 %all-reduce.7.cloned.1.call-done = f32[512,1024]{1,0:T(8,128)} async-done(((f32[512,1024]{1,0:T(8,128)}), f32[512,1024]{1,0:T(8,128)}) %all-reduce.7.cloned.1.call-update) | async-done | bytes 2097168 | tf_op jit(solution)/shard_map/psum | solution.py:79
  146.4 60.0 %all-gather.6.cloned.1.call-done = bf16[2,1024,1152]{2,1,0:T(8,128)(2,1)} async-done(((bf16[2,512,1152]{2,1,0:T(8,128)(2,1)}), bf16[2,1024,1152]{2,1,0:T(8,128)(2,1)}) %all-gather.6.cloned.1.call-update) | async-done | bytes 4718608 | tf_op jit(solution)/shard_map/all_gather | solution.py:59
  206.4 5.1 fusion.19
  214.4 29.5 %all-gather.8.cloned.1.call-done = bf16[1152,1024]{1,0:T(8,128)(2,1)} async-done(((bf16[1152,512]{1,0:T(8,128)(2,1)}), bf16[1152,1024]{1,0:T(8,128)(2,1)}) %all-gather.8.cloned.1.call-update) | async-done | bytes 2359312 | tf_op jit(solution)/shard_map/all_gather | solution.py:60
  243.9 6.7 multiply_convert_fusion
  250.6 4.1 fusion.18
  254.6 4.5 fusion.22
  259.4 4.9 fusion.62
  264.3 81.2 %all-reduce.9.cloned.1.call-done = f32[512,1024]{1,0:T(8,128)} async-done(((f32[512,1024]{1,0:T(8,128)}), f32[512,1024]{1,0:T(8,128)}) %all-reduce.9.cloned.1.call-update) | async-done | bytes 2097168 | tf_op jit(solution)/shard_map/psum | solution.py:101
  366.6 5.2 fusion.24
  376.7 4.3 pad_maximum_fusion
  381.3 131.5 %all-reduce.11.cloned.1.call-done = (f32[512,1024]{1,0:T(8,128)}, f32[512,1024]{1,0:T(8,128)}) async-done(((f32[512,1024]{1,0:T(8,128)}, f32[512,1024]{1,0:T(8,128)}), (f32[512,1024]{1,0:T(8,128)}, f32[512,1024]{1,0:T(8,128)})) %all-reduce.11.cloned.1.call-update) | async-done | bytes 4194320 | tf_op jit(solution)/shard_map/psum | solution.py:87
  516.2 18.3 %reduce-scatter.10.cloned.1.call-done = f32[256,512]{1,0:T(8,128)} async-done(((f32[256,1024]{1,0:T(8,128)}), f32[256,512]{1,0:T(8,128)}) %reduce-scatter.10.cloned.1.call-update) | async-done | bytes 524304 | tf_op jit(solution)/shard_map/reduce_scatter | solution.py:147
  534.4 45.7 %reduce-scatter.8.cloned.1.call-done = f32[3,512,256]{2,1,0:T(8,128)} async-done(((f32[3,1024,256]{2,1,0:T(8,128)}), f32[3,512,256]{2,1,0:T(8,128)}) %reduce-scatter.8.cloned.1.call-update) | async-done | bytes 1572880 | tf_op jit(solution)/shard_map/reduce_scatter | solution.py:146
  580.1 63.0 %reduce-scatter.14.cloned.1.call-done = f32[1152,512]{1,0:T(8,128)} async-done(((f32[1152,1024]{1,0:T(8,128)}), f32[1152,512]{1,0:T(8,128)}) %reduce-scatter.14.cloned.1.call-update) | async-done | bytes 2359312 | tf_op jit(solution)/shard_map/reduce_scatter | solution.py:149
  643.1 112.8 %reduce-scatter.12.cloned.1.call-done = f32[2,512,1152]{2,1,0:T(8,128)} async-done(((f32[2,1024,1152]{2,1,0:T(8,128)}), f32[2,512,1152]{2,1,0:T(8,128)}) %reduce-scatter.12.cloned.1.call-update) | async-done | bytes 4718608 | tf_op jit(solution)/shard_map/reduce_scatter | solution.py:148
  756.0 13.1 %psum.79 = f32[3,256]{1,0:T(4,128)} all-reduce(f32[3,256]{1,0:T(4,128)S(1)} %pad_maximum_fusion.5), channel_id=1, replica_groups=mesh['fsdp'=2,'context'=4,'tensor'=4] {'fsdp','context'}, use_global_device_ids=true, to_apply=%region_25.26 | all-reduce | flops 768 | bytes 6144 | tf_op jit(solution)/shard_map/psum | solution.py:153
  769.1 3.6 add_bitcast_fusion
  775.8 6.3 psum.78
  782.1 159.7 %all-reduce.13.cloned.1.call-done = (f32[3,512,256]{2,1,0:T(8,128)}, f32[256,512]{1,0:T(8,128)}, f32[2,512,1152]{2,1,0:T(8,128)}, f32[1152,512]{1,0:T(8,128)}) async-done(((f32[3,512,256]{2,1,0:T(8,128)}, f32[256,512]{1,0:T(8,128)}, f32[2,512,1152]{2,1,0:T(8,128)}, f32[1152,512]{1,0:T(8,128)}), (f32[3,512,256]{2,1,0:T(8,128)}, f32[256,512]{1,0:T(8,128)}, f32[2,512,1152]{2,1,0:T(8,128)}, ...) | async-done | bytes 9175056 | tf_op jit(solution)/shard_map/psum | solution.py:152
  945.3 5.0 copy.29
  (136 shorter events, 58.8 us)
Async XLA Ops:
  7.2 32.3 %all-gather.4.cloned.1.call-start = ((), (), s32[]{:S(2)}) async-start(), calls=%async_computation.5 | async-start | bytes 2359296 | tf_op jit(solution)/shard_map/all_gather | solution.py:57
  7.9 135.3 %all-reduce.7.cloned.1.call-start = ((), (), s32[]{:S(2)}) async-start(), calls=%async_computation.6 | async-start | bytes 4194304 | tf_op jit(solution)/shard_map/psum | solution.py:79
  15.0 26.4 %copy-start.2 = (bf16[1,512,1024]{2,1,0:T(8,128)(2,1)S(1)}, bf16[1,512,1024]{2,1,0:T(8,128)(2,1)}, u32[]{:S(2)}) copy-start(bf16[1,512,1024]{2,1,0:T(8,128)(2,1)} %param.9) | copy-start | bytes 3145732
  42.8 12.1 %copy-start.20 = (f32[512,256]{1,0:T(8,128)}, f32[512,256]{1,0:T(8,128)S(1)}, u32[]{:S(2)}) copy-start(f32[512,256]{1,0:T(8,128)S(1)} %get-tuple-element.43) | copy-start | bytes 1572868
  42.8 10.5 %collective-permute-start = (f32[2,256]{1,0:T(2,128)S(1)}, f32[2,256]{1,0:T(2,128)S(1)}, u32[]{:S(2)}, u32[]{:S(2)}) collective-permute-start(f32[2,256]{1,0:T(2,128)S(1)} %slice.98), channel_id=1, source_target_pairs={{0,4},{4,8},{8,12},{1,5},{5,9},{9,13},{2,6},{6,10},{10,14},{3,7},{... | collective-permute-start | bytes 6152 | tf_op jit(solution)/shard_map/ppermute | solution.py:12
  57.3 149.1 %all-gather.6.cloned.1.call-start = ((), (), s32[]{:S(2)}) async-start(), calls=%async_computation.7 | async-start | bytes 7077888 | tf_op jit(solution)/shard_map/all_gather | solution.py:59
  58.1 185.8 %all-gather.8.cloned.1.call-start = ((), (), s32[]{:S(2)}) async-start(), calls=%async_computation.8 | async-start | bytes 3538944 | tf_op jit(solution)/shard_map/all_gather | solution.py:60
  58.7 286.9 %all-reduce.9.cloned.1.call-start = ((), (), s32[]{:S(2)}) async-start(), calls=%async_computation.9 | async-start | bytes 4194304 | tf_op jit(solution)/shard_map/psum | solution.py:101
  206.4 5.1 copy-start.3
  206.4 5.1 copy-start.29
  250.5 4.1 copy-start.13
  250.5 4.1 copy-start.15
  259.2 253.6 %all-reduce.11.cloned.1.call-start = ((), (), s32[]{:S(2)}) async-start(), calls=%async_computation.15 | async-start | bytes 8388608 | tf_op jit(solution)/shard_map/psum | solution.py:87
  351.5 3.5 copy-start.19
  351.5 3.2 collective-permute-start.1
  358.1 176.3 %reduce-scatter.10.cloned.1.call-start = ((), (), s32[]{:S(2)}) async-start(), calls=%async_computation.11 | async-start | bytes 1572864 | tf_op jit(solution)/shard_map/reduce_scatter | solution.py:147
  361.4 218.7 %reduce-scatter.8.cloned.1.call-start = ((), (), s32[]{:S(2)}) async-start(), calls=%async_computation.10 | async-start | bytes 4718592 | tf_op jit(solution)/shard_map/reduce_scatter | solution.py:146
  366.5 276.6 %reduce-scatter.14.cloned.1.call-start = ((), (), s32[]{:S(2)}) async-start(), calls=%async_computation.13 | async-start | bytes 7077888 | tf_op jit(solution)/shard_map/reduce_scatter | solution.py:149
  371.8 384.2 %reduce-scatter.12.cloned.1.call-start = ((), (), s32[]{:S(2)}) async-start(), calls=%async_computation.12 | async-start | bytes 14155776 | tf_op jit(solution)/shard_map/reduce_scatter | solution.py:148
  381.0 393.7 %reduce-scatter.16.cloned.1.call-start = ((), (), s32[]{:S(2)}) async-start(), calls=%async_computation.14 | async-start | bytes 786432
  516.1 425.7 %all-reduce.13.cloned.1.call-start = ((), (), s32[]{:S(2)}) async-start(), calls=%async_computation.16 | async-start | bytes 18350080 | tf_op jit(solution)/shard_map/psum | solution.py:152
  769.1 3.6 copy-start.1
  769.1 3.6 copy-start.6
  945.3 5.0 copy-start.10
  (20 other events, 42.0 us)
Sparse Core Ops, SparseCore 0:
  9.5 29.8 all-gather.3
  57.5 85.6 all-reduce.6
  144.7 61.6 all-gather.5
  207.8 36.0 all-gather.7
  259.3 86.1 all-reduce.8
  358.2 154.5 all-reduce.10
  515.0 19.3 reduce-scatter.9
  536.7 43.3 reduce-scatter.7
  583.0 60.0 reduce-scatter.13
  645.3 110.6 reduce-scatter.11
  758.8 14.6 reduce-scatter.15
  776.1 165.6 all-reduce.12
where the time goes:
time: 959 us
  waiting for transfers between devices  811 us (85%)
  matrix products  54 us (6%)
  blocking collectives  33.8 us (4%)
  other arithmetic  23.9 us (2%)
  local copies, waits for them, and re-layouts  17 us (2%)
  between operations  14.6 us (2%)
    psum x1, waiting for transfers between devices, local(): lax.psum((pieces[0], pieces[1], pieces[2], pieces[3], pieces[4]), 'context')  160 us
    psum x1, waiting for transfers between devices, local(): lax.psum(matmul_plain(act_value, full_down), 'tensor')  131 us
    reduce_scatter x1, waiting for transfers between devices, local(): lax.psum_scatter(term_gate_up, 'fsdp', scatter_dimension=1, tiled=True)  113 us
    psum x1, waiting for transfers between devices, local(): first_sum = inputs + lax.psum(matmul_plain(gated, full_out), 'tensor')  84.5 us
    psum x1, waiting for transfers between devices, local(): lax.psum(matmul_right(grad_gate, full_gate_up[0]) + matmul_right(grad_up,...  81.2 us
    reduce_scatter x1, waiting for transfers between devices, local(): lax.psum_scatter(term_down, 'fsdp', scatter_dimension=1, tiled=True)  63 us
    all_gather x1, waiting for transfers between devices, local(): lax.all_gather(w_gate_up, 'fsdp', axis=1, tiled=True)  60 us
    reduce_scatter x1, waiting for transfers between devices, local(): lax.psum_scatter(term_in, 'fsdp', scatter_dimension=1, tiled=True)  45.7 us
  transfers between devices with their start and end apart: 14, of which 12 were waited for; matrix products, arithmetic and copies ran while one was open for 5% of the time, Pallas kernels for 0%

commit v1 on v0

--- a/solution.py
+++ b/solution.py
@@ -76,7 +76,7 @@
     back_two = extended[:-2] * keep_two
     conv_value = kernel_taps[2] * mixed + kernel_taps[1] * back_one + kernel_taps[0] * back_two
     gated = (c_part * conv_value).astype(jnp.bfloat16)
-    first_sum = inputs + lax.psum(matmul_plain(gated, full_out), "tensor")
+    first_sum = inputs + jnp.sum(lax.all_gather(matmul_plain(gated, full_out), "tensor"), axis=0)
     normed_two, root_two = norm_forward(first_sum)
     hidden_two = (normed_two * gain_second).astype(jnp.bfloat16)
     gate_value = matmul_plain(hidden_two, full_gate_up[0])

time: 959 us -> 1020 us (1.064)
  waiting for transfers between devices: 811 us -> 868 us
    all_gather x0 -> x1, waiting for transfers between devices: none -> 148 us  [local(): lax.all_gather(matmul_plain(gated, full_out), 'tensor')]
    psum x1 -> x0, waiting for transfers between devices: 84.5 us -> none  [local(): first_sum = inputs + lax.psum(matmul_plain(gated, full_out), 'tensor')]
  transfers between devices with their start and end apart: 14 -> 14, of which waited for: 12 -> 12; matrix products, arithmetic and copies ran while one was open for 5% -> 6% of each run, Pallas kernels for 0% -> 0%
where the time goes in v1:
time: 1020 us
  waiting for transfers between devices  868 us (85%)
  matrix products  53.8 us (5%)
  blocking collectives  33.9 us (3%)
  other arithmetic  30.1 us (3%)
  local copies, waits for them, and re-layouts  17.4 us (2%)
  between operations  14.5 us (1%)
    psum x1, waiting for transfers between devices, local(): lax.psum((pieces[0], pieces[1], pieces[2], pieces[3], pieces[4]), 'context')  160 us
    all_gather x1, waiting for transfers between devices, local(): lax.all_gather(matmul_plain(gated, full_out), 'tensor')  148 us
    psum x1, waiting for transfers between devices, local(): lax.psum(matmul_plain(act_value, full_down), 'tensor')  132 us
    reduce_scatter x1, waiting for transfers between devices, local(): lax.psum_scatter(term_gate_up, 'fsdp', scatter_dimension=1, tiled=True)  113 us
    psum x1, waiting for transfers between devices, local(): lax.psum(matmul_right(grad_gate, full_gate_up[0]) + matmul_right(grad_up,...  81.2 us
    reduce_scatter x1, waiting for transfers between devices, local(): lax.psum_scatter(term_down, 'fsdp', scatter_dimension=1, tiled=True)  63 us
    all_gather x1, waiting for transfers between devices, local(): lax.all_gather(w_gate_up, 'fsdp', axis=1, tiled=True)  52.3 us
    reduce_scatter x1, waiting for transfers between devices, local(): lax.psum_scatter(term_in, 'fsdp', scatter_dimension=1, tiled=True)  45.7 us
  transfers between devices with their start and end apart: 14, of which 12 were waited for; matrix products, arithmetic and copies ran while one was open for 6% of the time, Pallas kernels for 0%

profile of v1, /device:TPU:0, one launch (start us, length us, event | category | flops | bytes accessed | tf_op | source)
XLA Modules:
  0.0 1021.1 jit_solution(15162387970060687774)
XLA Ops:
  9.4 5.5 all_gather.25
  17.5 21.9 %all-gather.6.cloned.1.call-done = bf16[3,1024,256]{2,1,0:T(8,128)(2,1)} async-done(((bf16[3,512,256]{2,1,0:T(8,128)(2,1)}), bf16[3,1024,256]{2,1,0:T(8,128)(2,1)}) %all-gather.6.cloned.1.call-update) | async-done | bytes 1572880 | tf_op jit(solution)/shard_map/all_gather | solution.py:57
  44.3 8.9 all_gather.27
  58.7 147.9 %all-gather.12.cloned.1.call-done = f32[2048,1024]{1,0:T(8,128)} async-done(((f32[512,1024]{1,0:T(8,128)}), f32[2048,1024]{1,0:T(8,128)}) %all-gather.12.cloned.1.call-update) | async-done | bytes 8388624 | tf_op jit(solution)/shard_map/all_gather | solution.py:79
  206.6 5.9 reduce_sum.93
  216.7 52.3 %all-gather.8.cloned.1.call-done = bf16[2,1024,1152]{2,1,0:T(8,128)(2,1)} async-done(((bf16[2,512,1152]{2,1,0:T(8,128)(2,1)}), bf16[2,1024,1152]{2,1,0:T(8,128)(2,1)}) %all-gather.8.cloned.1.call-update) | async-done | bytes 4718608 | tf_op jit(solution)/shard_map/all_gather | solution.py:59
  269.0 5.1 fusion.22
  277.0 29.5 %all-gather.10.cloned.1.call-done = bf16[1152,1024]{1,0:T(8,128)(2,1)} async-done(((bf16[1152,512]{1,0:T(8,128)(2,1)}), bf16[1152,1024]{1,0:T(8,128)(2,1)}) %all-gather.10.cloned.1.call-update) | async-done | bytes 2359312 | tf_op jit(solution)/shard_map/all_gather | solution.py:60
  306.5 6.7 multiply_convert_fusion
  313.1 4.1 fusion.21
  317.2 4.5 fusion.25
  322.0 4.9 fusion.66
  326.9 81.2 %all-reduce.6.cloned.1.call-done = f32[512,1024]{1,0:T(8,128)} async-done(((f32[512,1024]{1,0:T(8,128)}), f32[512,1024]{1,0:T(8,128)}) %all-reduce.6.cloned.1.call-update) | async-done | bytes 2097168 | tf_op jit(solution)/shard_map/psum | solution.py:101
  429.1 5.2 fusion.28
  439.1 4.3 pad_maximum_fusion
  443.7 131.7 %all-reduce.8.cloned.1.call-done = (f32[512,1024]{1,0:T(8,128)}, f32[512,1024]{1,0:T(8,128)}) async-done(((f32[512,1024]{1,0:T(8,128)}, f32[512,1024]{1,0:T(8,128)}), (f32[512,1024]{1,0:T(8,128)}, f32[512,1024]{1,0:T(8,128)})) %all-reduce.8.cloned.1.call-update) | async-done | bytes 4194320 | tf_op jit(solution)/shard_map/psum | solution.py:87
  578.7 18.3 %reduce-scatter.10.cloned.1.call-done = f32[256,512]{1,0:T(8,128)} async-done(((f32[256,1024]{1,0:T(8,128)}), f32[256,512]{1,0:T(8,128)}) %reduce-scatter.10.cloned.1.call-update) | async-done | bytes 524304 | tf_op jit(solution)/shard_map/reduce_scatter | solution.py:147
  597.0 45.7 %reduce-scatter.8.cloned.1.call-done = f32[3,512,256]{2,1,0:T(8,128)} async-done(((f32[3,1024,256]{2,1,0:T(8,128)}), f32[3,512,256]{2,1,0:T(8,128)}) %reduce-scatter.8.cloned.1.call-update) | async-done | bytes 1572880 | tf_op jit(solution)/shard_map/reduce_scatter | solution.py:146
  642.7 63.0 %reduce-scatter.14.cloned.1.call-done = f32[1152,512]{1,0:T(8,128)} async-done(((f32[1152,1024]{1,0:T(8,128)}), f32[1152,512]{1,0:T(8,128)}) %reduce-scatter.14.cloned.1.call-update) | async-done | bytes 2359312 | tf_op jit(solution)/shard_map/reduce_scatter | solution.py:149
  705.7 112.8 %reduce-scatter.12.cloned.1.call-done = f32[2,512,1152]{2,1,0:T(8,128)} async-done(((f32[2,1024,1152]{2,1,0:T(8,128)}), f32[2,512,1152]{2,1,0:T(8,128)}) %reduce-scatter.12.cloned.1.call-update) | async-done | bytes 4718608 | tf_op jit(solution)/shard_map/reduce_scatter | solution.py:148
  818.5 13.1 %psum.71 = f32[3,256]{1,0:T(4,128)} all-reduce(f32[3,256]{1,0:T(4,128)S(1)} %pad_maximum_fusion.5), channel_id=1, replica_groups=mesh['fsdp'=2,'context'=4,'tensor'=4] {'fsdp','context'}, use_global_device_ids=true, to_apply=%region_25.26 | all-reduce | flops 768 | bytes 6144 | tf_op jit(solution)/shard_map/psum | solution.py:153
  838.1 6.4 psum.70
  844.5 159.9 %all-reduce.10.cloned.1.call-done = (f32[3,512,256]{2,1,0:T(8,128)}, f32[256,512]{1,0:T(8,128)}, f32[2,512,1152]{2,1,0:T(8,128)}, f32[1152,512]{1,0:T(8,128)}) async-done(((f32[3,512,256]{2,1,0:T(8,128)}, f32[256,512]{1,0:T(8,128)}, f32[2,512,1152]{2,1,0:T(8,128)}, f32[1152,512]{1,0:T(8,128)}), (f32[3,512,256]{2,1,0:T(8,128)}, f32[256,512]{1,0:T(8,128)}, f32[2,512,1152]{2,1,0:T(8,128)}, ...) | async-done | bytes 9175056 | tf_op jit(solution)/shard_map/psum | solution.py:152
  1007.9 5.0 copy.28
  (137 shorter events, 63.0 us)
Async XLA Ops:
  7.2 32.3 %all-gather.6.cloned.1.call-start = ((), (), s32[]{:S(2)}) async-start(), calls=%async_computation.5 | async-start | bytes 2359296 | tf_op jit(solution)/shard_map/all_gather | solution.py:57
  7.9 198.7 %all-gather.12.cloned.1.call-start = ((), (), s32[]{:S(2)}) async-start(), calls=%async_computation.13 | async-start | bytes 10485760 | tf_op jit(solution)/shard_map/all_gather | solution.py:79
  15.0 26.4 %copy-start.2 = (bf16[1,512,1024]{2,1,0:T(8,128)(2,1)S(1)}, bf16[1,512,1024]{2,1,0:T(8,128)(2,1)}, u32[]{:S(2)}) copy-start(bf16[1,512,1024]{2,1,0:T(8,128)(2,1)} %param.9) | copy-start | bytes 3145732
  41.5 11.8 %copy-start.20 = (f32[512,256]{1,0:T(8,128)}, f32[512,256]{1,0:T(8,128)S(1)}, u32[]{:S(2)}) copy-start(f32[512,256]{1,0:T(8,128)S(1)} %fusion.50) | copy-start | bytes 1572868
  42.8 12.1 %copy-start.17 = (f32[512,256]{1,0:T(8,128)}, f32[512,256]{1,0:T(8,128)S(1)}, u32[]{:S(2)}) copy-start(f32[512,256]{1,0:T(8,128)S(1)} %get-tuple-element.43) | copy-start | bytes 1572868
  42.8 10.5 %collective-permute-start = (f32[2,256]{1,0:T(2,128)S(1)}, f32[2,256]{1,0:T(2,128)S(1)}, u32[]{:S(2)}, u32[]{:S(2)}) collective-permute-start(f32[2,256]{1,0:T(2,128)S(1)} %slice.98), channel_id=1, source_target_pairs={{0,4},{4,8},{8,12},{1,5},{5,9},{9,13},{2,6},{6,10},{10,14},{3,7},{... | collective-permute-start | bytes 6152 | tf_op jit(solution)/shard_map/ppermute | solution.py:12
  57.3 211.7 %all-gather.8.cloned.1.call-start = ((), (), s32[]{:S(2)}) async-start(), calls=%async_computation.6 | async-start | bytes 7077888 | tf_op jit(solution)/shard_map/all_gather | solution.py:59
  58.1 248.4 %all-gather.10.cloned.1.call-start = ((), (), s32[]{:S(2)}) async-start(), calls=%async_computation.7 | async-start | bytes 3538944 | tf_op jit(solution)/shard_map/all_gather | solution.py:60
  58.6 349.5 %all-reduce.6.cloned.1.call-start = ((), (), s32[]{:S(2)}) async-start(), calls=%async_computation.8 | async-start | bytes 4194304 | tf_op jit(solution)/shard_map/psum | solution.py:101
  269.0 5.1 copy-start.12
  269.0 5.1 copy-start.26
  313.1 4.1 copy-start.27
  313.1 4.1 copy-start.29
  321.8 253.6 %all-reduce.8.cloned.1.call-start = ((), (), s32[]{:S(2)}) async-start(), calls=%async_computation.15 | async-start | bytes 8388608 | tf_op jit(solution)/shard_map/psum | solution.py:87
  414.1 3.5 copy-start.16
  414.1 3.2 collective-permute-start.1
  420.7 176.3 %reduce-scatter.10.cloned.1.call-start = ((), (), s32[]{:S(2)}) async-start(), calls=%async_computation.10 | async-start | bytes 1572864 | tf_op jit(solution)/shard_map/reduce_scatter | solution.py:147
  424.0 218.7 %reduce-scatter.8.cloned.1.call-start = ((), (), s32[]{:S(2)}) async-start(), calls=%async_computation.9 | async-start | bytes 4718592 | tf_op jit(solution)/shard_map/reduce_scatter | solution.py:146
  429.1 276.6 %reduce-scatter.14.cloned.1.call-start = ((), (), s32[]{:S(2)}) async-start(), calls=%async_computation.12 | async-start | bytes 7077888 | tf_op jit(solution)/shard_map/reduce_scatter | solution.py:149
  434.3 384.2 %reduce-scatter.12.cloned.1.call-start = ((), (), s32[]{:S(2)}) async-start(), calls=%async_computation.11 | async-start | bytes 14155776 | tf_op jit(solution)/shard_map/reduce_scatter | solution.py:148
  443.4 393.7 %reduce-scatter.16.cloned.1.call-start = ((), (), s32[]{:S(2)}) async-start(), calls=%async_computation.14 | async-start | bytes 786432
  578.7 425.7 %all-reduce.10.cloned.1.call-start = ((), (), s32[]{:S(2)}) async-start(), calls=%async_computation.16 | async-start | bytes 18350080 | tf_op jit(solution)/shard_map/psum | solution.py:152
  831.7 3.5 copy-start.5
  1007.9 5.0 copy-start.9
  (20 other events, 43.4 us)
Sparse Core Ops, SparseCore 0:
  9.5 29.8 all-gather.5
  57.4 149.1 all-gather.11
  208.2 60.8 all-gather.7
  270.4 36.0 all-gather.9
  321.9 86.1 all-reduce.5
  420.8 154.4 all-reduce.7
  577.6 19.3 reduce-scatter.9
  599.2 43.3 reduce-scatter.7
  645.6 60.0 reduce-scatter.13
  707.8 110.6 reduce-scatter.11
  821.3 14.6 reduce-scatter.15
  838.7 165.6 all-reduce.9
